TPU v7x, 32 devices: a whole 2x2x4 slice. The times are simulated.
32 devices in a mesh: groups: 2 (over x), inner: 16 (over z, y, core).
Axes of the slice: x: 2, y: 2, z: 4, core: 2. Of those that a mesh axis runs over, the one named last changes fastest.
Arguments:
- hidden_rows: bfloat16 [2048, 2048], P(('groups', 'inner')), parts along dimension 0, may hold values from -6 to 6
- token_embed: bfloat16 [2048, 2048], P(('groups', 'inner')), parts along dimension 0, may hold values from -6 to 6
- first_routes: int32 [2048, 8], P(('groups', 'inner')), parts along dimension 0, may hold values from 0 to 15, all different within a row; in each aligned block of 64 rows (0 to 63, 64 to 127, ...) at most 48 rows name the same one
- first_gates: float32 [2048, 8], P(('groups', 'inner')), parts along dimension 0, may hold values from 0.2 to 0.6
- first_gate_up: bfloat16 [16, 2048, 1024], P('inner'), may hold values from -0.125 to 0.125
- first_down: bfloat16 [16, 512, 2048], P('inner'), may hold values from -0.25 to 0.25
- second_routes: int32 [2048, 8], P(('groups', 'inner')), parts along dimension 0, may hold values from 0 to 15, all different within a row; in each aligned block of 64 rows (0 to 63, 64 to 127, ...) at most 48 rows name the same one
- second_gates: float32 [2048, 8], P(('groups', 'inner')), parts along dimension 0, may hold values from 0.2 to 0.6
- second_gate_up: bfloat16 [16, 2048, 1024], P('inner'), may hold values from -0.125 to 0.125
- second_down: bfloat16 [16, 512, 2048], P('inner'), may hold values from -0.25 to 0.25
- hidden_gain: float32 [2048], replicated, may hold values from 0.25 to 1.75
- embed_gain: float32 [2048], replicated, may hold values from 0.25 to 1.75
- merge_weight: bfloat16 [4096, 2048], P('inner'), may hold values from -0.09375 to 0.09375
Outputs:
- final_rows: bfloat16 [2048, 2048], P(('groups', 'inner')), parts along dimension 0
There are 2 independent parts, one for each index of `groups`. A program takes and returns all parts, laid end to end along the dimension named above; an argument that names none is the same for every part. Nothing has to cross between parts.
Inputs may be any that keep to these rules, and one draw needn't show every extreme that they name: `first_routes`: among the 64 tokens of one block, no expert is named more than 48 times, and in every draw some expert is named exactly 48 times in some block. `second_routes`: among the 64 tokens of one block, no expert is named more than 48 times, and in every draw some expert is named exactly 48 times in some block.
All inputs are finite; a program needn't handle non-finite values.
Results may differ from a plain program's by a relative error of at most 0.01.
Values may be sent and summed in bfloat16 or wider, within the bound.
A program may use at most 128 MiB of HBM per device.

v0:
```python
import jax
import jax.numpy as jnp
from jax import lax
from jax.sharding import PartitionSpec as P

EPSILON = 1e-06


def rms_scale(values, gain_vec):
    widened = values.astype(jnp.float32)
    inverse_rms = lax.rsqrt(jnp.mean(widened * widened, axis=-1, keepdims=True) + EPSILON)
    return (widened * inverse_rms * gain_vec).astype(jnp.bfloat16)


def dense_gates(routes, gates, experts):
    hit = routes[:, :, None] == jnp.arange(experts, dtype=jnp.int32)[None, None, :]
    return jnp.sum(jnp.where(hit, gates[:, :, None], 0.0), axis=1)


def dense_layer(rows, gate_column, gate_up, down):
    everyone = lax.all_gather(rows, "inner", axis=0, tiled=True)
    width = down.shape[0]
    projected = jnp.dot(everyone, gate_up, preferred_element_type=jnp.float32)
    inner = (jax.nn.silu(projected[:, :width]) * projected[:, width:]).astype(jnp.bfloat16)
    out = jnp.dot(inner, down, preferred_element_type=jnp.float32)
    share = jnp.where(gate_column > 0, out * gate_column, 0.0).astype(jnp.bfloat16)
    return lax.psum_scatter(share, "inner", scatter_dimension=0, tiled=True).astype(jnp.float32)


def local(
    hidden_rows,
    token_embed,
    first_routes,
    first_gates,
    first_gate_up,
    first_down,
    second_routes,
    second_gates,
    second_gate_up,
    second_down,
    hidden_gain,
    embed_gain,
    merge_weight,
):
    experts = lax.axis_size("inner")
    me = lax.axis_index("inner")
    both = jnp.concatenate(
        [
            dense_gates(first_routes, first_gates, experts),
            dense_gates(second_routes, second_gates, experts),
        ],
        axis=1,
    )
    both = lax.all_gather(both, "inner", axis=0, tiled=True)
    first_column = lax.dynamic_slice_in_dim(both, me, 1, axis=1)
    second_column = lax.dynamic_slice_in_dim(both, me + experts, 1, axis=1)
    first_moe = dense_layer(hidden_rows, first_column, first_gate_up[0], first_down[0])
    after_first = (hidden_rows.astype(jnp.float32) + first_moe).astype(jnp.bfloat16)
    merged_in = jnp.concatenate(
        [rms_scale(after_first, hidden_gain), rms_scale(token_embed, embed_gain)], axis=1
    )
    columns = lax.all_to_all(merged_in, "inner", split_axis=1, concat_axis=0, tiled=True)
    partial = jnp.dot(columns, merge_weight, preferred_element_type=jnp.float32)
    merged = lax.psum_scatter(
        partial.astype(jnp.bfloat16), "inner", scatter_dimension=0, tiled=True
    ).astype(jnp.float32)
    after_merge = (after_first.astype(jnp.float32) + jax.nn.silu(merged)).astype(jnp.bfloat16)
    second_moe = dense_layer(after_merge, second_column, second_gate_up[0], second_down[0])
    return (after_merge.astype(jnp.float32) + second_moe).astype(jnp.bfloat16)


def solution(mesh):
    rows = P(("groups", "inner"), None)
    return jax.shard_map(
        local,
        mesh=mesh,
        in_specs=(
            rows,
            rows,
            rows,
            rows,
            P("inner", None, None),
            P("inner", None, None),
            rows,
            rows,
            P("inner", None, None),
            P("inner", None, None),
            P(),
            P(),
            P("inner", None),
        ),
        out_specs=rows,
        check_vma=False,
    )
```

profile of v0, /device:TPU:0, one launch (start us, length us, event | category | flops | bytes accessed | tf_op | source)
XLA Modules:
  0.0 384.9 jit_solution(18183789587168572780)
XLA Ops:
  6.5 0.0 copy-start
  6.5 0.0 all-gather.4.cloned.1.call-start
  6.5 0.7 all-gather.4.cloned.1.call-update
  7.3 0.0 reduce-scatter.4.cloned.1.call-start
  7.3 0.8 select_reduce_fusion
  8.1 24.3 %all-gather = f32[16,64,32]{1,2,0:T(8,128)S(1)} all-gather(f32[1,64,32]{1,2,0:T(8,128)S(1)} %maximum_bitcast_fusion), channel_id=1, replica_groups=mesh['groups'=2,'inner'=16] {'inner'}, dimensions={0}, use_global_device_ids=true | all-gather | bytes 139264 | tf_op jit(solution)/shard_map/all_gather | solution.py:54
  32.3 0.2 copy.34
  32.5 0.1 reshape.26
  32.7 30.4 %all-gather.4.cloned.1.call-done = bf16[1024,2048]{1,0:T(8,128)(2,1)} async-done(((bf16[64,2048]{1,0:T(8,128)(2,1)}), bf16[1024,2048]{1,0:T(8,128)(2,1)}) %all-gather.4.cloned.1.call-update) | async-done | bytes 4194320 | tf_op jit(solution)/shard_map/all_gather | solution.py:21
  63.1 7.5 %fusion.2 = f32[1024,1024]{1,0:T(8,128)S(1)} fusion(bf16[1024,2048]{1,0:T(8,128)(2,1)} %all-gather.4.cloned.1.call-done, bf16[1,2048,1024]{2,1,0:T(8,128)(2,1)} %param.17), kind=kOutput, calls=%fused_computation.4 | convolution fusion | flops 4294967296 | bytes 12582912 | tf_op jit(solution)/shard_map/dot_general | solution.py:23
  70.6 0.0 copy-done
  70.6 4.1 %select_convert_fusion.1 = bf16[1024,2048]{1,0:T(8,128)(2,1)} fusion(f32[1024]{0:T(1024)S(1)} %bitcast.33, pred[1024]{0:T(1024)(128)(4,1)S(1)} %get-tuple-element.5, bf16[1,512,2048]{2,1,0:T(8,128)(2,1)S(1)} %copy-done, f32[1024,1024]{1,0:T(8,128)S(1)} %fusion.2), kind=kOutput, calls=%fused_computation.1 | convolution fusion | flops 2156920832 | bytes 10490880 | tf_op jit(solution)/shard_map/dot_general | solution.py:25
  74.7 0.0 copy-start.4
  74.7 0.0 copy-start.6
  74.7 0.0 copy-start.1
  74.7 0.0 copy-start.7
  74.7 0.0 reduce-scatter.4.cloned.1.call-update
  74.8 0.0 reduce-scatter.6.cloned.1.call-start
  74.8 0.9 copy-done.4
  75.7 0.2 fusion.12
  75.8 0.0 copy-done.6
  75.8 0.1 fusion.14
  76.0 70.2 %reduce-scatter.4.cloned.1.call-done = bf16[64,2048]{1,0:T(8,128)(2,1)} async-done(((bf16[1024,2048]{1,0:T(8,128)(2,1)}), bf16[64,2048]{1,0:T(8,128)(2,1)}) %reduce-scatter.4.cloned.1.call-update) | async-done | bytes 262160 | tf_op jit(solution)/shard_map/reduce_scatter | solution.py:27
  146.2 0.0 copy-done.1
  146.2 0.0 copy-start.5
  146.2 1.2 fusion.18
  147.5 0.0 copy-done.7
  147.5 1.1 fusion.20
  148.7 17.8 %all_to_all.19 = bf16[64,16,256]{2,0,1:T(8,128)(2,1)S(1)} all-to-all(bf16[64,16,256]{2,0,1:T(8,128)(2,1)S(1)} %bitcast.31), channel_id=1, replica_groups=mesh['groups'=2,'inner'=16] {'inner'}, dimensions={1} | all-to-all | bytes 1048576 | tf_op jit(solution)/shard_map/all_to_all | solution.py:62
  166.5 0.0 copy-done.5
  166.5 0.0 copy-start.3
  166.5 3.2 convolution_convert_fusion
  169.7 0.0 reduce-scatter.6.cloned.1.call-update
  169.7 0.0 all-gather.6.cloned.1.call-start
  169.7 72.4 %reduce-scatter.6.cloned.1.call-done = bf16[64,2048]{1,0:T(8,128)(2,1)} async-done(((bf16[1024,2048]{1,0:T(8,128)(2,1)}), bf16[64,2048]{1,0:T(8,128)(2,1)}) %reduce-scatter.6.cloned.1.call-update) | async-done | bytes 262160 | tf_op jit(solution)/shard_map/reduce_scatter | solution.py:64
  242.1 0.0 copy-done.3
  242.1 1.8 fusion.21
  244.0 0.0 all-gather.6.cloned.1.call-update
  244.0 0.0 reduce-scatter.8.cloned.1.call-start
  244.0 49.4 %all-gather.6.cloned.1.call-done = bf16[1024,2048]{1,0:T(8,128)(2,1)} async-done(((bf16[64,2048]{1,0:T(8,128)(2,1)}), bf16[1024,2048]{1,0:T(8,128)(2,1)}) %all-gather.6.cloned.1.call-update) | async-done | bytes 4194320 | tf_op jit(solution)/shard_map/all_gather | solution.py:21
  293.5 0.0 copy-start.8
  293.5 7.6 %fusion = f32[1024,1024]{1,0:T(8,128)S(1)} fusion(bf16[1024,2048]{1,0:T(8,128)(2,1)} %all-gather.6.cloned.1.call-done, bf16[1,2048,1024]{2,1,0:T(8,128)(2,1)} %param.21), kind=kOutput, calls=%fused_computation.2 | convolution fusion | flops 4294967296 | bytes 12582912 | tf_op jit(solution)/shard_map/dot_general | solution.py:23
  301.1 0.0 copy-done.8
  301.1 4.1 %select_convert_fusion = bf16[1024,2048]{1,0:T(8,128)(2,1)} fusion(f32[1024]{0:T(1024)S(1)} %bitcast.32, pred[1024]{0:T(1024)(128)(4,1)S(1)} %get-tuple-element.9, bf16[1,512,2048]{2,1,0:T(8,128)(2,1)S(1)} %copy-done.8, f32[1024,1024]{1,0:T(8,128)S(1)} %fusion), kind=kOutput, calls=%fused_computation | convolution fusion | flops 2156920832 | bytes 10490880 | tf_op jit(solution)/shard_map/dot_general | solution.py:25
  305.2 0.0 reduce-scatter.8.cloned.1.call-update
  305.2 71.4 %reduce-scatter.8.cloned.1.call-done = bf16[64,2048]{1,0:T(8,128)(2,1)} async-done(((bf16[1024,2048]{1,0:T(8,128)(2,1)}), bf16[64,2048]{1,0:T(8,128)(2,1)}) %reduce-scatter.8.cloned.1.call-update) | async-done | bytes 262160 | tf_op jit(solution)/shard_map/reduce_scatter | solution.py:27
  376.7 0.0 copy-done.2
  376.7 1.7 add_convert_fusion
  (7 shorter events, 0.1 us)
Async XLA Ops:
  6.5 64.1 %copy-start = (bf16[1,512,2048]{2,1,0:T(8,128)(2,1)S(1)}, bf16[1,512,2048]{2,1,0:T(8,128)(2,1)}, u32[]{:S(2)}) copy-start(bf16[1,512,2048]{2,1,0:T(8,128)(2,1)} %param.18) | copy-start | bytes 6291460
  6.5 56.6 %all-gather.4.cloned.1.call-start = ((), (), s32[]{:S(2)}) async-start(), calls=%async_computation.4 | async-start | bytes 4456448 | tf_op jit(solution)/shard_map/all_gather | solution.py:21
  7.3 139.0 %reduce-scatter.4.cloned.1.call-start = ((), (), s32[]{:S(2)}) async-start(), calls=%async_computation.5 | async-start | bytes 4456448 | tf_op jit(solution)/shard_map/reduce_scatter | solution.py:27
  74.7 0.9 copy-start.4
  74.7 1.1 copy-start.6
  74.7 71.5 %copy-start.1 = (bf16[64,2048]{1,0:T(8,128)(2,1)S(1)}, bf16[64,2048]{1,0:T(8,128)(2,1)}, u32[]{:S(2)}) copy-start(bf16[64,2048]{1,0:T(8,128)(2,1)} %param.13) | copy-start | bytes 786436
  74.7 72.7 %copy-start.7 = (f32[2048]{0:T(1024)S(1)}, f32[2048]{0:T(1024)}, u32[]{:S(2)}) copy-start(f32[2048]{0:T(1024)} %param.23) | copy-start | bytes 24580
  74.8 167.4 %reduce-scatter.6.cloned.1.call-start = ((), (), s32[]{:S(2)}) async-start(), calls=%async_computation.6 | async-start | bytes 4456448 | tf_op jit(solution)/shard_map/reduce_scatter | solution.py:64
  146.2 20.3 %copy-start.5 = (bf16[256,2048]{1,0:T(8,128)(2,1)S(1)}, bf16[256,2048]{1,0:T(8,128)(2,1)}, u32[]{:S(2)}) copy-start(bf16[256,2048]{1,0:T(8,128)(2,1)} %param.25) | copy-start | bytes 3145732
  166.5 75.6 %copy-start.3 = (bf16[64,2048]{1,0:T(8,128)(2,1)S(1)}, bf16[64,2048]{1,0:T(8,128)(2,1)}, u32[]{:S(2)}) copy-start(bf16[64,2048]{1,0:T(8,128)(2,1)} %reduce-scatter.4.cloned.1.call-done) | copy-start | bytes 786436
  169.7 123.8 %all-gather.6.cloned.1.call-start = ((), (), s32[]{:S(2)}) async-start(), calls=%async_computation.7 | async-start | bytes 4456448 | tf_op jit(solution)/shard_map/all_gather | solution.py:21
  244.0 132.7 %reduce-scatter.8.cloned.1.call-start = ((), (), s32[]{:S(2)}) async-start(), calls=%async_computation.8 | async-start | bytes 4456448 | tf_op jit(solution)/shard_map/reduce_scatter | solution.py:27
  293.5 7.7 %copy-start.8 = (bf16[1,512,2048]{2,1,0:T(8,128)(2,1)S(1)}, bf16[1,512,2048]{2,1,0:T(8,128)(2,1)}, u32[]{:S(2)}) copy-start(bf16[1,512,2048]{2,1,0:T(8,128)(2,1)} %param.22) | copy-start | bytes 6291460
  305.2 71.5 %copy-start.2 = (bf16[64,2048]{1,0:T(8,128)(2,1)S(1)}, bf16[64,2048]{1,0:T(8,128)(2,1)}, u32[]{:S(2)}) copy-start(bf16[64,2048]{1,0:T(8,128)(2,1)} %fusion.21) | copy-start | bytes 786436
Sparse Core Ops, SparseCore 0:
  9.5 53.5 all-gather.3
  74.9 71.2 reduce-scatter.3
  169.8 72.2 reduce-scatter.5
  244.1 49.2 all-gather.5
  305.4 71.2 reduce-scatter.7
where the time goes:
time: 385 us
  waiting for transfers between devices  295 us (77%)
  blocking collectives  42.1 us (11%)
  matrix products  26.5 us (7%)
  between operations  13.2 us (3%)
  other arithmetic  7.03 us (2%)
    reduce_scatter x2, waiting for transfers between devices, dense_layer(): lax.psum_scatter(share, 'inner', scatter_dimension=0, tiled=True)  142 us
    all_gather x2, waiting for transfers between devices, dense_layer(): everyone = lax.all_gather(rows, 'inner', axis=0, tiled=True)  79.8 us
    reduce_scatter x1, waiting for transfers between devices, local(): lax.psum_scatter(partial.astype(jnp.bfloat16), 'inner', scatter_dimension...  72.4 us
    all_gather x1, blocking collectives, local(): both = lax.all_gather(both, 'inner', axis=0, tiled=True)  24.3 us
    all_to_all x1, blocking collectives, local(): lax.all_to_all(merged_in, 'inner', split_axis=1, concat_axis=0, tiled=True)  17.8 us
    dot_general x2, matrix products, dense_layer(): projected = jnp.dot(everyone, gate_up, preferred_element_type=jnp.float32)  15.1 us
    dot_general x2, matrix products, dense_layer(): out = jnp.dot(inner, down, preferred_element_type=jnp.float32)  8.21 us
  transfers between devices with their start and end apart: 5, of which 5 were waited for; matrix products, arithmetic and copies ran while one was open for 0% of the time, Pallas kernels for 0%

commit v1 on v0

--- a/solution.py
+++ b/solution.py
@@ -18,7 +18,14 @@
 
 
 def dense_layer(rows, gate_column, gate_up, down):
-    everyone = lax.all_gather(rows, "inner", axis=0, tiled=True)
+    ring = [rows]
+    for hop in range(15):
+        ring.append(lax.ppermute(ring[-1], "inner", [(dev, (dev + 1) % 16) for dev in range(16)]))
+    everyone = jnp.roll(
+        jnp.concatenate(ring[::-1], axis=0),
+        (lax.axis_index("inner") + 1) * ring[0].shape[0],
+        axis=0,
+    )
     width = down.shape[0]
     projected = jnp.dot(everyone, gate_up, preferred_element_type=jnp.float32)
     inner = (jax.nn.silu(projected[:, :width]) * projected[:, width:]).astype(jnp.bfloat16)

time: 385 us -> 556 us (1.44)
  waiting for transfers between devices: 295 us -> 459 us
  local copies, waits for them, and re-layouts: 1.22 us -> 16.3 us
    ppermute x0 -> x30, waiting for transfers between devices: none -> 246 us  [dense_layer(): lax.ppermute(ring[-1], 'inner', [(dev, (dev + 1) % 16) for dev in range(1...]
    all_gather x2 -> x0, waiting for transfers between devices: 79.8 us -> none  [dense_layer(): everyone = lax.all_gather(rows, 'inner', axis=0, tiled=True)]
    unnamed x19 -> x79, local copies, waits for them, and re-layouts: 1.02 us -> 16.1 us
  transfers between devices with their start and end apart: 5 -> 33, of which waited for: 5 -> 32; matrix products, arithmetic and copies ran while one was open for 0% -> 0% of each run, Pallas kernels for 0% -> 0%
where the time goes in v1:
time: 556 us; the launch traced here: 555 us
  waiting for transfers between devices  459 us (83%)
  blocking collectives  36.8 us (7%)
  matrix products  22.7 us (4%)
  local copies, waits for them, and re-layouts  16.3 us (3%)
  between operations  13.6 us (2%)
  other arithmetic  6.39 us (1%)
    ppermute x30, waiting for transfers between devices, dense_layer(): lax.ppermute(ring[-1], 'inner', [(dev, (dev + 1) % 16) for dev in range(1...  246 us
    reduce_scatter x2, waiting for transfers between devices, dense_layer(): lax.psum_scatter(share, 'inner', scatter_dimension=0, tiled=True)  140 us
    reduce_scatter x1, waiting for transfers between devices, local(): lax.psum_scatter(partial.astype(jnp.bfloat16), 'inner', scatter_dimension...  72.5 us
    all_gather x1, blocking collectives, local(): both = lax.all_gather(both, 'inner', axis=0, tiled=True)  19 us
    all_to_all x1, blocking collectives, local(): lax.all_to_all(merged_in, 'inner', split_axis=1, concat_axis=0, tiled=True)  17.8 us
    unnamed x79, local copies, waits for them, and re-layouts  16.1 us
    dot_general x2, matrix products, dense_layer(): projected = jnp.dot(everyone, gate_up, preferred_element_type=jnp.float32)  11.2 us
  transfers between devices with their start and end apart: 33, of which 32 were waited for; matrix products, arithmetic and copies ran while one was open for 0% of the time, Pallas kernels for 0%

profile of v1, /device:TPU:0, one launch (start us, length us, event | category | flops | bytes accessed | tf_op | source)
XLA Modules:
  0.0 555.5 jit_solution(3511299859143148977)
XLA Ops:
  7.0 9.2 %collective-permute-done = bf16[64,2048]{1,0:T(8,128)(2,1)S(1)} collective-permute-done((bf16[64,2048]{1,0:T(8,128)(2,1)}, bf16[64,2048]{1,0:T(8,128)(2,1)S(1)}, u32[]{:S(2)}, u32[]{:S(2)}) %collective-permute-start) | collective-permute-done | bytes 262176 | tf_op jit(solution)/shard_map/ppermute | solution.py:23
  16.3 8.5 %collective-permute-done.1 = bf16[64,2048]{1,0:T(8,128)(2,1)S(1)} collective-permute-done((bf16[64,2048]{1,0:T(8,128)(2,1)S(1)}, bf16[64,2048]{1,0:T(8,128)(2,1)S(1)}, u32[]{:S(2)}, u32[]{:S(2)}) %collective-permute-start.1) | collective-permute-done | bytes 262176 | tf_op jit(solution)/shard_map/ppermute | solution.py:23
  24.8 8.5 %collective-permute-done.2 = bf16[64,2048]{1,0:T(8,128)(2,1)S(1)} collective-permute-done((bf16[64,2048]{1,0:T(8,128)(2,1)S(1)}, bf16[64,2048]{1,0:T(8,128)(2,1)S(1)}, u32[]{:S(2)}, u32[]{:S(2)}) %collective-permute-start.2) | collective-permute-done | bytes 262176 | tf_op jit(solution)/shard_map/ppermute | solution.py:23
  33.3 8.5 %collective-permute-done.3 = bf16[64,2048]{1,0:T(8,128)(2,1)S(1)} collective-permute-done((bf16[64,2048]{1,0:T(8,128)(2,1)S(1)}, bf16[64,2048]{1,0:T(8,128)(2,1)S(1)}, u32[]{:S(2)}, u32[]{:S(2)}) %collective-permute-start.3) | collective-permute-done | bytes 262176 | tf_op jit(solution)/shard_map/ppermute | solution.py:23
  42.5 8.5 %collective-permute-done.4 = bf16[64,2048]{1,0:T(8,128)(2,1)S(1)} collective-permute-done((bf16[64,2048]{1,0:T(8,128)(2,1)S(1)}, bf16[64,2048]{1,0:T(8,128)(2,1)S(1)}, u32[]{:S(2)}, u32[]{:S(2)}) %collective-permute-start.4) | collective-permute-done | bytes 262176 | tf_op jit(solution)/shard_map/ppermute | solution.py:23
  51.7 8.5 %collective-permute-done.5 = bf16[64,2048]{1,0:T(8,128)(2,1)S(1)} collective-permute-done((bf16[64,2048]{1,0:T(8,128)(2,1)S(1)}, bf16[64,2048]{1,0:T(8,128)(2,1)S(1)}, u32[]{:S(2)}, u32[]{:S(2)}) %collective-permute-start.5) | collective-permute-done | bytes 262176 | tf_op jit(solution)/shard_map/ppermute | solution.py:23
  60.9 8.5 %collective-permute-done.6 = bf16[64,2048]{1,0:T(8,128)(2,1)S(1)} collective-permute-done((bf16[64,2048]{1,0:T(8,128)(2,1)S(1)}, bf16[64,2048]{1,0:T(8,128)(2,1)S(1)}, u32[]{:S(2)}, u32[]{:S(2)}) %collective-permute-start.6) | collective-permute-done | bytes 262176 | tf_op jit(solution)/shard_map/ppermute | solution.py:23
  70.1 8.5 %collective-permute-done.7 = bf16[64,2048]{1,0:T(8,128)(2,1)S(1)} collective-permute-done((bf16[64,2048]{1,0:T(8,128)(2,1)S(1)}, bf16[64,2048]{1,0:T(8,128)(2,1)S(1)}, u32[]{:S(2)}, u32[]{:S(2)}) %collective-permute-start.7) | collective-permute-done | bytes 262176 | tf_op jit(solution)/shard_map/ppermute | solution.py:23
  79.2 8.5 %collective-permute-done.8 = bf16[64,2048]{1,0:T(8,128)(2,1)S(1)} collective-permute-done((bf16[64,2048]{1,0:T(8,128)(2,1)S(1)}, bf16[64,2048]{1,0:T(8,128)(2,1)S(1)}, u32[]{:S(2)}, u32[]{:S(2)}) %collective-permute-start.8) | collective-permute-done | bytes 262176 | tf_op jit(solution)/shard_map/ppermute | solution.py:23
  88.4 8.5 %collective-permute-done.9 = bf16[64,2048]{1,0:T(8,128)(2,1)S(1)} collective-permute-done((bf16[64,2048]{1,0:T(8,128)(2,1)S(1)}, bf16[64,2048]{1,0:T(8,128)(2,1)S(1)}, u32[]{:S(2)}, u32[]{:S(2)}) %collective-permute-start.9) | collective-permute-done | bytes 262176 | tf_op jit(solution)/shard_map/ppermute | solution.py:23
  97.6 8.5 %collective-permute-done.10 = bf16[64,2048]{1,0:T(8,128)(2,1)S(1)} collective-permute-done((bf16[64,2048]{1,0:T(8,128)(2,1)S(1)}, bf16[64,2048]{1,0:T(8,128)(2,1)S(1)}, u32[]{:S(2)}, u32[]{:S(2)}) %collective-permute-start.10) | collective-permute-done | bytes 262176 | tf_op jit(solution)/shard_map/ppermute | solution.py:23
  106.8 8.5 %collective-permute-done.11 = bf16[64,2048]{1,0:T(8,128)(2,1)S(1)} collective-permute-done((bf16[64,2048]{1,0:T(8,128)(2,1)S(1)}, bf16[64,2048]{1,0:T(8,128)(2,1)S(1)}, u32[]{:S(2)}, u32[]{:S(2)}) %collective-permute-start.11) | collective-permute-done | bytes 262176 | tf_op jit(solution)/shard_map/ppermute | solution.py:23
  116.0 8.5 %collective-permute-done.12 = bf16[64,2048]{1,0:T(8,128)(2,1)S(1)} collective-permute-done((bf16[64,2048]{1,0:T(8,128)(2,1)S(1)}, bf16[64,2048]{1,0:T(8,128)(2,1)S(1)}, u32[]{:S(2)}, u32[]{:S(2)}) %collective-permute-start.12) | collective-permute-done | bytes 262176 | tf_op jit(solution)/shard_map/ppermute | solution.py:23
  125.4 7.7 %collective-permute-done.13 = bf16[64,2048]{1,0:T(8,128)(2,1)} collective-permute-done((bf16[64,2048]{1,0:T(8,128)(2,1)S(1)}, bf16[64,2048]{1,0:T(8,128)(2,1)}, u32[]{:S(2)}, u32[]{:S(2)}) %collective-permute-start.13) | collective-permute-done | bytes 262176 | tf_op jit(solution)/shard_map/ppermute | solution.py:23
  133.1 19.0 %all-gather = f32[16,64,32]{1,2,0:T(8,128)S(1)} all-gather(f32[1,64,32]{1,2,0:T(8,128)S(1)} %maximum_bitcast_fusion), channel_id=1, replica_groups=mesh['groups'=2,'inner'=16] {'inner'}, dimensions={0}, use_global_device_ids=true | all-gather | bytes 139264 | tf_op jit(solution)/shard_map/all_gather | solution.py:61
  152.5 1.1 constant_dynamic-update-slice_fusion.15
  153.6 1.4 constant_dynamic-update-slice_fusion.14
  155.0 1.0 constant_dynamic-update-slice_fusion.13
  157.0 1.0 constant_dynamic-update-slice_fusion.11
  159.9 1.0 constant_dynamic-update-slice_fusion.8
  161.1 5.6 %fusion.4 = f32[1024,1024]{1,0:T(8,128)S(1)} fusion(s32[]{:T(128)S(6)} %select_n.39, bf16[1024,2048]{1,0:T(8,128)(2,1)S(1)} %constant_dynamic-update-slice_fusion, bf16[1,2048,1024]{2,1,0:T(8,128)(2,1)S(1)} %copy-done.21), kind=kOutput, calls=%fused_computation.9 | convolution fusion | flops 4303355904 | bytes 12582916 | tf_op jit(solution)/shard_map/dot_general | solution.py:30
  166.8 4.2 select_convert_fusion.1
  172.2 70.1 %reduce-scatter.4.cloned.1.call-done = bf16[64,2048]{1,0:T(8,128)(2,1)} async-done(((bf16[1024,2048]{1,0:T(8,128)(2,1)}), bf16[64,2048]{1,0:T(8,128)(2,1)}) %reduce-scatter.4.cloned.1.call-update) | async-done | bytes 262160 | tf_op jit(solution)/shard_map/reduce_scatter | solution.py:34
  242.3 1.2 fusion.22
  243.5 1.1 fusion.24
  244.7 17.8 %all_to_all.19 = bf16[64,16,256]{2,0,1:T(8,128)(2,1)S(1)} all-to-all(bf16[64,16,256]{2,0,1:T(8,128)(2,1)S(1)} %bitcast.29), channel_id=1, replica_groups=mesh['groups'=2,'inner'=16] {'inner'}, dimensions={1} | all-to-all | bytes 1048576 | tf_op jit(solution)/shard_map/all_to_all | solution.py:69
  262.5 3.2 convolution_convert_fusion
  265.8 72.5 %reduce-scatter.6.cloned.1.call-done = bf16[64,2048]{1,0:T(8,128)(2,1)} async-done(((bf16[1024,2048]{1,0:T(8,128)(2,1)}), bf16[64,2048]{1,0:T(8,128)(2,1)}) %reduce-scatter.6.cloned.1.call-update) | async-done | bytes 262160 | tf_op jit(solution)/shard_map/reduce_scatter | solution.py:71
  338.3 1.1 fusion.25
  339.5 8.5 %collective-permute-done.15 = bf16[64,2048]{1,0:T(8,128)(2,1)S(1)} collective-permute-done((bf16[64,2048]{1,0:T(8,128)(2,1)S(1)}, bf16[64,2048]{1,0:T(8,128)(2,1)S(1)}, u32[]{:S(2)}, u32[]{:S(2)}) %collective-permute-start.15) | collective-permute-done | bytes 262176 | tf_op jit(solution)/shard_map/ppermute | solution.py:23
  348.0 8.5 %collective-permute-done.16 = bf16[64,2048]{1,0:T(8,128)(2,1)S(1)} collective-permute-done((bf16[64,2048]{1,0:T(8,128)(2,1)S(1)}, bf16[64,2048]{1,0:T(8,128)(2,1)S(1)}, u32[]{:S(2)}, u32[]{:S(2)}) %collective-permute-start.16) | collective-permute-done | bytes 262176 | tf_op jit(solution)/shard_map/ppermute | solution.py:23
  356.5 8.5 %collective-permute-done.17 = bf16[64,2048]{1,0:T(8,128)(2,1)S(1)} collective-permute-done((bf16[64,2048]{1,0:T(8,128)(2,1)S(1)}, bf16[64,2048]{1,0:T(8,128)(2,1)S(1)}, u32[]{:S(2)}, u32[]{:S(2)}) %collective-permute-start.17) | collective-permute-done | bytes 262176 | tf_op jit(solution)/shard_map/ppermute | solution.py:23
  365.0 8.5 %collective-permute-done.18 = bf16[64,2048]{1,0:T(8,128)(2,1)S(1)} collective-permute-done((bf16[64,2048]{1,0:T(8,128)(2,1)S(1)}, bf16[64,2048]{1,0:T(8,128)(2,1)S(1)}, u32[]{:S(2)}, u32[]{:S(2)}) %collective-permute-start.18) | collective-permute-done | bytes 262176 | tf_op jit(solution)/shard_map/ppermute | solution.py:23
  373.5 8.5 %collective-permute-done.19 = bf16[64,2048]{1,0:T(8,128)(2,1)S(1)} collective-permute-done((bf16[64,2048]{1,0:T(8,128)(2,1)S(1)}, bf16[64,2048]{1,0:T(8,128)(2,1)S(1)}, u32[]{:S(2)}, u32[]{:S(2)}) %collective-permute-start.19) | collective-permute-done | bytes 262176 | tf_op jit(solution)/shard_map/ppermute | solution.py:23
  382.0 8.5 %collective-permute-done.20 = bf16[64,2048]{1,0:T(8,128)(2,1)S(1)} collective-permute-done((bf16[64,2048]{1,0:T(8,128)(2,1)S(1)}, bf16[64,2048]{1,0:T(8,128)(2,1)S(1)}, u32[]{:S(2)}, u32[]{:S(2)}) %collective-permute-start.20) | collective-permute-done | bytes 262176 | tf_op jit(solution)/shard_map/ppermute | solution.py:23
  390.5 8.5 %collective-permute-done.21 = bf16[64,2048]{1,0:T(8,128)(2,1)S(1)} collective-permute-done((bf16[64,2048]{1,0:T(8,128)(2,1)S(1)}, bf16[64,2048]{1,0:T(8,128)(2,1)S(1)}, u32[]{:S(2)}, u32[]{:S(2)}) %collective-permute-start.21) | collective-permute-done | bytes 262176 | tf_op jit(solution)/shard_map/ppermute | solution.py:23
  399.0 8.5 %collective-permute-done.22 = bf16[64,2048]{1,0:T(8,128)(2,1)S(1)} collective-permute-done((bf16[64,2048]{1,0:T(8,128)(2,1)S(1)}, bf16[64,2048]{1,0:T(8,128)(2,1)S(1)}, u32[]{:S(2)}, u32[]{:S(2)}) %collective-permute-start.22) | collective-permute-done | bytes 262176 | tf_op jit(solution)/shard_map/ppermute | solution.py:23
  407.4 8.5 %collective-permute-done.23 = bf16[64,2048]{1,0:T(8,128)(2,1)S(1)} collective-permute-done((bf16[64,2048]{1,0:T(8,128)(2,1)S(1)}, bf16[64,2048]{1,0:T(8,128)(2,1)S(1)}, u32[]{:S(2)}, u32[]{:S(2)}) %collective-permute-start.23) | collective-permute-done | bytes 262176 | tf_op jit(solution)/shard_map/ppermute | solution.py:23
  415.9 8.5 %collective-permute-done.24 = bf16[64,2048]{1,0:T(8,128)(2,1)S(1)} collective-permute-done((bf16[64,2048]{1,0:T(8,128)(2,1)S(1)}, bf16[64,2048]{1,0:T(8,128)(2,1)S(1)}, u32[]{:S(2)}, u32[]{:S(2)}) %collective-permute-start.24) | collective-permute-done | bytes 262176 | tf_op jit(solution)/shard_map/ppermute | solution.py:23
  424.4 8.5 %collective-permute-done.25 = bf16[64,2048]{1,0:T(8,128)(2,1)S(1)} collective-permute-done((bf16[64,2048]{1,0:T(8,128)(2,1)S(1)}, bf16[64,2048]{1,0:T(8,128)(2,1)S(1)}, u32[]{:S(2)}, u32[]{:S(2)}) %collective-permute-start.25) | collective-permute-done | bytes 262176 | tf_op jit(solution)/shard_map/ppermute | solution.py:23
  432.9 8.5 %collective-permute-done.26 = bf16[64,2048]{1,0:T(8,128)(2,1)S(1)} collective-permute-done((bf16[64,2048]{1,0:T(8,128)(2,1)S(1)}, bf16[64,2048]{1,0:T(8,128)(2,1)S(1)}, u32[]{:S(2)}, u32[]{:S(2)}) %collective-permute-start.26) | collective-permute-done | bytes 262176 | tf_op jit(solution)/shard_map/ppermute | solution.py:23
  441.4 8.5 %collective-permute-done.27 = bf16[64,2048]{1,0:T(8,128)(2,1)S(1)} collective-permute-done((bf16[64,2048]{1,0:T(8,128)(2,1)S(1)}, bf16[64,2048]{1,0:T(8,128)(2,1)S(1)}, u32[]{:S(2)}, u32[]{:S(2)}) %collective-permute-start.27) | collective-permute-done | bytes 262176 | tf_op jit(solution)/shard_map/ppermute | solution.py:23
  449.9 8.5 %collective-permute-done.28 = bf16[64,2048]{1,0:T(8,128)(2,1)S(1)} collective-permute-done((bf16[64,2048]{1,0:T(8,128)(2,1)S(1)}, bf16[64,2048]{1,0:T(8,128)(2,1)S(1)}, u32[]{:S(2)}, u32[]{:S(2)}) %collective-permute-start.28) | collective-permute-done | bytes 262176 | tf_op jit(solution)/shard_map/ppermute | solution.py:23
  458.4 8.5 %collective-permute-done.29 = bf16[64,2048]{1,0:T(8,128)(2,1)S(1)} collective-permute-done((bf16[64,2048]{1,0:T(8,128)(2,1)S(1)}, bf16[64,2048]{1,0:T(8,128)(2,1)S(1)}, u32[]{:S(2)}, u32[]{:S(2)}) %collective-permute-start.29) | collective-permute-done | bytes 262176 | tf_op jit(solution)/shard_map/ppermute | solution.py:23
  467.4 5.5 fusion.1
  472.9 4.2 select_convert_fusion
  477.1 70.2 %reduce-scatter.8.cloned.1.call-done = bf16[64,2048]{1,0:T(8,128)(2,1)} async-done(((bf16[1024,2048]{1,0:T(8,128)(2,1)}), bf16[64,2048]{1,0:T(8,128)(2,1)}) %reduce-scatter.8.cloned.1.call-update) | async-done | bytes 262160 | tf_op jit(solution)/shard_map/reduce_scatter | solution.py:34
  547.3 1.7 add_convert_fusion
  (123 shorter events, 12.9 us)
Async XLA Ops:
  6.5 160.2 %copy-start = (bf16[1,512,2048]{2,1,0:T(8,128)(2,1)S(1)}, bf16[1,512,2048]{2,1,0:T(8,128)(2,1)}, u32[]{:S(2)}) copy-start(bf16[1,512,2048]{2,1,0:T(8,128)(2,1)} %param.20) | copy-start | bytes 6291460
  6.5 235.7 %reduce-scatter.4.cloned.1.call-start = ((), (), s32[]{:S(2)}) async-start(), calls=%async_computation.4 | async-start | bytes 4456448 | tf_op jit(solution)/shard_map/reduce_scatter | solution.py:34
  6.5 9.7 %collective-permute-start = (bf16[64,2048]{1,0:T(8,128)(2,1)}, bf16[64,2048]{1,0:T(8,128)(2,1)S(1)}, u32[]{:S(2)}, u32[]{:S(2)}) collective-permute-start(bf16[64,2048]{1,0:T(8,128)(2,1)} %param.15), channel_id=1, source_target_pairs={{0,1},{1,2},{2,3},{3,4},{4,5},{5,6},{6,7},{7,8},{8,9},{9,10},{10,1... | collective-permute-start | bytes 786440 | tf_op jit(solution)/shard_map/ppermute | solution.py:23
  16.3 8.5 %collective-permute-start.1 = (bf16[64,2048]{1,0:T(8,128)(2,1)S(1)}, bf16[64,2048]{1,0:T(8,128)(2,1)S(1)}, u32[]{:S(2)}, u32[]{:S(2)}) collective-permute-start(bf16[64,2048]{1,0:T(8,128)(2,1)S(1)} %collective-permute-done), channel_id=1, source_target_pairs={{0,1},{1,2},{2,3},{3,4},{4,5},{5,6},{6,7},{7,8},{8,9},{9,10},{10,1... | collective-permute-start | bytes 786440 | tf_op jit(solution)/shard_map/ppermute | solution.py:23
  24.8 8.5 %collective-permute-start.2 = (bf16[64,2048]{1,0:T(8,128)(2,1)S(1)}, bf16[64,2048]{1,0:T(8,128)(2,1)S(1)}, u32[]{:S(2)}, u32[]{:S(2)}) collective-permute-start(bf16[64,2048]{1,0:T(8,128)(2,1)S(1)} %collective-permute-done.1), channel_id=1, source_target_pairs={{0,1},{1,2},{2,3},{3,4},{4,5},{5,6},{6,7},{7,8},{8,9},{9,10},{10,1... | collective-permute-start | bytes 786440 | tf_op jit(solution)/shard_map/ppermute | solution.py:23
  33.3 8.5 %collective-permute-start.3 = (bf16[64,2048]{1,0:T(8,128)(2,1)S(1)}, bf16[64,2048]{1,0:T(8,128)(2,1)S(1)}, u32[]{:S(2)}, u32[]{:S(2)}) collective-permute-start(bf16[64,2048]{1,0:T(8,128)(2,1)S(1)} %collective-permute-done.2), channel_id=1, source_target_pairs={{0,1},{1,2},{2,3},{3,4},{4,5},{5,6},{6,7},{7,8},{8,9},{9,10},{10,1... | collective-permute-start | bytes 786440 | tf_op jit(solution)/shard_map/ppermute | solution.py:23
  42.5 8.5 %collective-permute-start.4 = (bf16[64,2048]{1,0:T(8,128)(2,1)S(1)}, bf16[64,2048]{1,0:T(8,128)(2,1)S(1)}, u32[]{:S(2)}, u32[]{:S(2)}) collective-permute-start(bf16[64,2048]{1,0:T(8,128)(2,1)S(1)} %collective-permute-done.3), channel_id=1, source_target_pairs={{0,1},{1,2},{2,3},{3,4},{4,5},{5,6},{6,7},{7,8},{8,9},{9,10},{10,1... | collective-permute-start | bytes 786440 | tf_op jit(solution)/shard_map/ppermute | solution.py:23
  51.7 8.5 %collective-permute-start.5 = (bf16[64,2048]{1,0:T(8,128)(2,1)S(1)}, bf16[64,2048]{1,0:T(8,128)(2,1)S(1)}, u32[]{:S(2)}, u32[]{:S(2)}) collective-permute-start(bf16[64,2048]{1,0:T(8,128)(2,1)S(1)} %collective-permute-done.4), channel_id=1, source_target_pairs={{0,1},{1,2},{2,3},{3,4},{4,5},{5,6},{6,7},{7,8},{8,9},{9,10},{10,1... | collective-permute-start | bytes 786440 | tf_op jit(solution)/shard_map/ppermute | solution.py:23
  60.9 8.5 %collective-permute-start.6 = (bf16[64,2048]{1,0:T(8,128)(2,1)S(1)}, bf16[64,2048]{1,0:T(8,128)(2,1)S(1)}, u32[]{:S(2)}, u32[]{:S(2)}) collective-permute-start(bf16[64,2048]{1,0:T(8,128)(2,1)S(1)} %collective-permute-done.5), channel_id=1, source_target_pairs={{0,1},{1,2},{2,3},{3,4},{4,5},{5,6},{6,7},{7,8},{8,9},{9,10},{10,1... | collective-permute-start | bytes 786440 | tf_op jit(solution)/shard_map/ppermute | solution.py:23
  70.1 8.5 %collective-permute-start.7 = (bf16[64,2048]{1,0:T(8,128)(2,1)S(1)}, bf16[64,2048]{1,0:T(8,128)(2,1)S(1)}, u32[]{:S(2)}, u32[]{:S(2)}) collective-permute-start(bf16[64,2048]{1,0:T(8,128)(2,1)S(1)} %collective-permute-done.6), channel_id=1, source_target_pairs={{0,1},{1,2},{2,3},{3,4},{4,5},{5,6},{6,7},{7,8},{8,9},{9,10},{10,1... | collective-permute-start | bytes 786440 | tf_op jit(solution)/shard_map/ppermute | solution.py:23
  79.2 8.5 %collective-permute-start.8 = (bf16[64,2048]{1,0:T(8,128)(2,1)S(1)}, bf16[64,2048]{1,0:T(8,128)(2,1)S(1)}, u32[]{:S(2)}, u32[]{:S(2)}) collective-permute-start(bf16[64,2048]{1,0:T(8,128)(2,1)S(1)} %collective-permute-done.7), channel_id=1, source_target_pairs={{0,1},{1,2},{2,3},{3,4},{4,5},{5,6},{6,7},{7,8},{8,9},{9,10},{10,1... | collective-permute-start | bytes 786440 | tf_op jit(solution)/shard_map/ppermute | solution.py:23
  88.4 8.5 %collective-permute-start.9 = (bf16[64,2048]{1,0:T(8,128)(2,1)S(1)}, bf16[64,2048]{1,0:T(8,128)(2,1)S(1)}, u32[]{:S(2)}, u32[]{:S(2)}) collective-permute-start(bf16[64,2048]{1,0:T(8,128)(2,1)S(1)} %collective-permute-done.8), channel_id=1, source_target_pairs={{0,1},{1,2},{2,3},{3,4},{4,5},{5,6},{6,7},{7,8},{8,9},{9,10},{10,1... | collective-permute-start | bytes 786440 | tf_op jit(solution)/shard_map/ppermute | solution.py:23
  97.6 8.5 %collective-permute-start.10 = (bf16[64,2048]{1,0:T(8,128)(2,1)S(1)}, bf16[64,2048]{1,0:T(8,128)(2,1)S(1)}, u32[]{:S(2)}, u32[]{:S(2)}) collective-permute-start(bf16[64,2048]{1,0:T(8,128)(2,1)S(1)} %collective-permute-done.9), channel_id=1, source_target_pairs={{0,1},{1,2},{2,3},{3,4},{4,5},{5,6},{6,7},{7,8},{8,9},{9,10},{10,1... | collective-permute-start | bytes 786440 | tf_op jit(solution)/shard_map/ppermute | solution.py:23
  106.8 8.5 %collective-permute-start.11 = (bf16[64,2048]{1,0:T(8,128)(2,1)S(1)}, bf16[64,2048]{1,0:T(8,128)(2,1)S(1)}, u32[]{:S(2)}, u32[]{:S(2)}) collective-permute-start(bf16[64,2048]{1,0:T(8,128)(2,1)S(1)} %collective-permute-done.10), channel_id=1, source_target_pairs={{0,1},{1,2},{2,3},{3,4},{4,5},{5,6},{6,7},{7,8},{8,9},{9,10},{10,1... | collective-permute-start | bytes 786440 | tf_op jit(solution)/shard_map/ppermute | solution.py:23
  116.0 8.5 %collective-permute-start.12 = (bf16[64,2048]{1,0:T(8,128)(2,1)S(1)}, bf16[64,2048]{1,0:T(8,128)(2,1)S(1)}, u32[]{:S(2)}, u32[]{:S(2)}) collective-permute-start(bf16[64,2048]{1,0:T(8,128)(2,1)S(1)} %collective-permute-done.11), channel_id=1, source_target_pairs={{0,1},{1,2},{2,3},{3,4},{4,5},{5,6},{6,7},{7,8},{8,9},{9,10},{10,1... | collective-permute-start | bytes 786440 | tf_op jit(solution)/shard_map/ppermute | solution.py:23
  124.5 27.6 %copy-start.18 = (bf16[64,2048]{1,0:T(8,128)(2,1)}, bf16[64,2048]{1,0:T(8,128)(2,1)S(1)}, u32[]{:S(2)}) copy-start(bf16[64,2048]{1,0:T(8,128)(2,1)S(1)} %collective-permute-done.12) | copy-start | bytes 786436
  124.5 8.6 %collective-permute-start.13 = (bf16[64,2048]{1,0:T(8,128)(2,1)S(1)}, bf16[64,2048]{1,0:T(8,128)(2,1)}, u32[]{:S(2)}, u32[]{:S(2)}) collective-permute-start(bf16[64,2048]{1,0:T(8,128)(2,1)S(1)} %collective-permute-done.12), channel_id=1, source_target_pairs={{0,1},{1,2},{2,3},{3,4},{4,5},{5,6},{6,7},{7,8},{8,9},{9,10},{10,1... | collective-permute-start | bytes 786440 | tf_op jit(solution)/shard_map/ppermute | solution.py:23
  133.1 19.4 %collective-permute-start.14 = (bf16[64,2048]{1,0:T(8,128)(2,1)}, bf16[64,2048]{1,0:T(8,128)(2,1)}, u32[]{:S(2)}, u32[]{:S(2)}) collective-permute-start(bf16[64,2048]{1,0:T(8,128)(2,1)} %collective-permute-done.13), channel_id=1, source_target_pairs={{0,1},{1,2},{2,3},{3,4},{4,5},{5,6},{6,7},{7,8},{8,9},{9,10},{10,1... | collective-permute-start | bytes 786440 | tf_op jit(solution)/shard_map/ppermute | solution.py:23
  152.3 8.8 %copy-start.1 = (bf16[64,2048]{1,0:T(8,128)(2,1)S(1)}, bf16[64,2048]{1,0:T(8,128)(2,1)}, u32[]{:S(2)}) copy-start(bf16[64,2048]{1,0:T(8,128)(2,1)} %param.15) | copy-start | bytes 786436
  152.4 8.6 %copy-start.6 = (bf16[64,2048]{1,0:T(8,128)(2,1)S(1)}, bf16[64,2048]{1,0:T(8,128)(2,1)}, u32[]{:S(2)}) copy-start(bf16[64,2048]{1,0:T(8,128)(2,1)} %copy-done.5) | copy-start | bytes 786436
  152.4 8.4 %copy-start.12 = (bf16[64,2048]{1,0:T(8,128)(2,1)S(1)}, bf16[64,2048]{1,0:T(8,128)(2,1)}, u32[]{:S(2)}) copy-start(bf16[64,2048]{1,0:T(8,128)(2,1)} %copy-done.11) | copy-start | bytes 786436
  152.4 8.5 %copy-start.10 = (bf16[64,2048]{1,0:T(8,128)(2,1)S(1)}, bf16[64,2048]{1,0:T(8,128)(2,1)}, u32[]{:S(2)}) copy-start(bf16[64,2048]{1,0:T(8,128)(2,1)} %copy-done.9) | copy-start | bytes 786436
  152.4 8.5 %copy-start.8 = (bf16[64,2048]{1,0:T(8,128)(2,1)S(1)}, bf16[64,2048]{1,0:T(8,128)(2,1)}, u32[]{:S(2)}) copy-start(bf16[64,2048]{1,0:T(8,128)(2,1)} %copy-done.7) | copy-start | bytes 786436
  152.5 8.6 %copy-start.21 = (bf16[1,2048,1024]{2,1,0:T(8,128)(2,1)S(1)}, bf16[1,2048,1024]{2,1,0:T(8,128)(2,1)}, u32[]{:S(2)}) copy-start(bf16[1,2048,1024]{2,1,0:T(8,128)(2,1)} %param.19) | copy-start | bytes 12582916
  170.9 0.9 copy-start.3
  170.9 1.1 copy-start.19
  170.9 72.6 %copy-start.20 = (f32[2048]{0:T(1024)S(1)}, f32[2048]{0:T(1024)}, u32[]{:S(2)}) copy-start(f32[2048]{0:T(1024)} %param.25) | copy-start | bytes 24580
  171.0 167.3 %reduce-scatter.6.cloned.1.call-start = ((), (), s32[]{:S(2)}) async-start(), calls=%async_computation.5 | async-start | bytes 4456448 | tf_op jit(solution)/shard_map/reduce_scatter | solution.py:71
  242.3 20.2 %copy-start.4 = (bf16[256,2048]{1,0:T(8,128)(2,1)S(1)}, bf16[256,2048]{1,0:T(8,128)(2,1)}, u32[]{:S(2)}) copy-start(bf16[256,2048]{1,0:T(8,128)(2,1)} %param.27) | copy-start | bytes 3145732
  262.5 75.8 %copy-start.2 = (bf16[64,2048]{1,0:T(8,128)(2,1)S(1)}, bf16[64,2048]{1,0:T(8,128)(2,1)}, u32[]{:S(2)}) copy-start(bf16[64,2048]{1,0:T(8,128)(2,1)} %reduce-scatter.4.cloned.1.call-done) | copy-start | bytes 786436
  265.8 281.5 %reduce-scatter.8.cloned.1.call-start = ((), (), s32[]{:S(2)}) async-start(), calls=%async_computation.6 | async-start | bytes 4456448 | tf_op jit(solution)/shard_map/reduce_scatter | solution.py:34
  339.4 127.9 %copy-start.22 = (bf16[1,2048,1024]{2,1,0:T(8,128)(2,1)S(1)}, bf16[1,2048,1024]{2,1,0:T(8,128)(2,1)}, u32[]{:S(2)}) copy-start(bf16[1,2048,1024]{2,1,0:T(8,128)(2,1)} %param.23) | copy-start | bytes 12582916
  339.4 8.5 %collective-permute-start.15 = (bf16[64,2048]{1,0:T(8,128)(2,1)S(1)}, bf16[64,2048]{1,0:T(8,128)(2,1)S(1)}, u32[]{:S(2)}, u32[]{:S(2)}) collective-permute-start(bf16[64,2048]{1,0:T(8,128)(2,1)S(1)} %fusion.25), channel_id=1, source_target_pairs={{0,1},{1,2},{2,3},{3,4},{4,5},{5,6},{6,7},{7,8},{8,9},{9,10},{10,1... | collective-permute-start | bytes 786440 | tf_op jit(solution)/shard_map/ppermute | solution.py:23
  348.0 8.5 %collective-permute-start.16 = (bf16[64,2048]{1,0:T(8,128)(2,1)S(1)}, bf16[64,2048]{1,0:T(8,128)(2,1)S(1)}, u32[]{:S(2)}, u32[]{:S(2)}) collective-permute-start(bf16[64,2048]{1,0:T(8,128)(2,1)S(1)} %collective-permute-done.15), channel_id=1, source_target_pairs={{0,1},{1,2},{2,3},{3,4},{4,5},{5,6},{6,7},{7,8},{8,9},{9,10},{10,1... | collective-permute-start | bytes 786440 | tf_op jit(solution)/shard_map/ppermute | solution.py:23
  356.5 8.5 %collective-permute-start.17 = (bf16[64,2048]{1,0:T(8,128)(2,1)S(1)}, bf16[64,2048]{1,0:T(8,128)(2,1)S(1)}, u32[]{:S(2)}, u32[]{:S(2)}) collective-permute-start(bf16[64,2048]{1,0:T(8,128)(2,1)S(1)} %collective-permute-done.16), channel_id=1, source_target_pairs={{0,1},{1,2},{2,3},{3,4},{4,5},{5,6},{6,7},{7,8},{8,9},{9,10},{10,1... | collective-permute-start | bytes 786440 | tf_op jit(solution)/shard_map/ppermute | solution.py:23
  365.0 8.5 %collective-permute-start.18 = (bf16[64,2048]{1,0:T(8,128)(2,1)S(1)}, bf16[64,2048]{1,0:T(8,128)(2,1)S(1)}, u32[]{:S(2)}, u32[]{:S(2)}) collective-permute-start(bf16[64,2048]{1,0:T(8,128)(2,1)S(1)} %collective-permute-done.17), channel_id=1, source_target_pairs={{0,1},{1,2},{2,3},{3,4},{4,5},{5,6},{6,7},{7,8},{8,9},{9,10},{10,1... | collective-permute-start | bytes 786440 | tf_op jit(solution)/shard_map/ppermute | solution.py:23
  373.5 8.5 %collective-permute-start.19 = (bf16[64,2048]{1,0:T(8,128)(2,1)S(1)}, bf16[64,2048]{1,0:T(8,128)(2,1)S(1)}, u32[]{:S(2)}, u32[]{:S(2)}) collective-permute-start(bf16[64,2048]{1,0:T(8,128)(2,1)S(1)} %collective-permute-done.18), channel_id=1, source_target_pairs={{0,1},{1,2},{2,3},{3,4},{4,5},{5,6},{6,7},{7,8},{8,9},{9,10},{10,1... | collective-permute-start | bytes 786440 | tf_op jit(solution)/shard_map/ppermute | solution.py:23
  382.0 8.5 %collective-permute-start.20 = (bf16[64,2048]{1,0:T(8,128)(2,1)S(1)}, bf16[64,2048]{1,0:T(8,128)(2,1)S(1)}, u32[]{:S(2)}, u32[]{:S(2)}) collective-permute-start(bf16[64,2048]{1,0:T(8,128)(2,1)S(1)} %collective-permute-done.19), channel_id=1, source_target_pairs={{0,1},{1,2},{2,3},{3,4},{4,5},{5,6},{6,7},{7,8},{8,9},{9,10},{10,1... | collective-permute-start | bytes 786440 | tf_op jit(solution)/shard_map/ppermute | solution.py:23
  390.5 8.5 %collective-permute-start.21 = (bf16[64,2048]{1,0:T(8,128)(2,1)S(1)}, bf16[64,2048]{1,0:T(8,128)(2,1)S(1)}, u32[]{:S(2)}, u32[]{:S(2)}) collective-permute-start(bf16[64,2048]{1,0:T(8,128)(2,1)S(1)} %collective-permute-done.20), channel_id=1, source_target_pairs={{0,1},{1,2},{2,3},{3,4},{4,5},{5,6},{6,7},{7,8},{8,9},{9,10},{10,1... | collective-permute-start | bytes 786440 | tf_op jit(solution)/shard_map/ppermute | solution.py:23
  398.9 8.5 %collective-permute-start.22 = (bf16[64,2048]{1,0:T(8,128)(2,1)S(1)}, bf16[64,2048]{1,0:T(8,128)(2,1)S(1)}, u32[]{:S(2)}, u32[]{:S(2)}) collective-permute-start(bf16[64,2048]{1,0:T(8,128)(2,1)S(1)} %collective-permute-done.21), channel_id=1, source_target_pairs={{0,1},{1,2},{2,3},{3,4},{4,5},{5,6},{6,7},{7,8},{8,9},{9,10},{10,1... | collective-permute-start | bytes 786440 | tf_op jit(solution)/shard_map/ppermute | solution.py:23
  407.4 8.5 %collective-permute-start.23 = (bf16[64,2048]{1,0:T(8,128)(2,1)S(1)}, bf16[64,2048]{1,0:T(8,128)(2,1)S(1)}, u32[]{:S(2)}, u32[]{:S(2)}) collective-permute-start(bf16[64,2048]{1,0:T(8,128)(2,1)S(1)} %collective-permute-done.22), channel_id=1, source_target_pairs={{0,1},{1,2},{2,3},{3,4},{4,5},{5,6},{6,7},{7,8},{8,9},{9,10},{10,1... | collective-permute-start | bytes 786440 | tf_op jit(solution)/shard_map/ppermute | solution.py:23
  415.9 8.5 %collective-permute-start.24 = (bf16[64,2048]{1,0:T(8,128)(2,1)S(1)}, bf16[64,2048]{1,0:T(8,128)(2,1)S(1)}, u32[]{:S(2)}, u32[]{:S(2)}) collective-permute-start(bf16[64,2048]{1,0:T(8,128)(2,1)S(1)} %collective-permute-done.23), channel_id=1, source_target_pairs={{0,1},{1,2},{2,3},{3,4},{4,5},{5,6},{6,7},{7,8},{8,9},{9,10},{10,1... | collective-permute-start | bytes 786440 | tf_op jit(solution)/shard_map/ppermute | solution.py:23
  424.4 8.5 %collective-permute-start.25 = (bf16[64,2048]{1,0:T(8,128)(2,1)S(1)}, bf16[64,2048]{1,0:T(8,128)(2,1)S(1)}, u32[]{:S(2)}, u32[]{:S(2)}) collective-permute-start(bf16[64,2048]{1,0:T(8,128)(2,1)S(1)} %collective-permute-done.24), channel_id=1, source_target_pairs={{0,1},{1,2},{2,3},{3,4},{4,5},{5,6},{6,7},{7,8},{8,9},{9,10},{10,1... | collective-permute-start | bytes 786440 | tf_op jit(solution)/shard_map/ppermute | solution.py:23
  432.9 8.5 %collective-permute-start.26 = (bf16[64,2048]{1,0:T(8,128)(2,1)S(1)}, bf16[64,2048]{1,0:T(8,128)(2,1)S(1)}, u32[]{:S(2)}, u32[]{:S(2)}) collective-permute-start(bf16[64,2048]{1,0:T(8,128)(2,1)S(1)} %collective-permute-done.25), channel_id=1, source_target_pairs={{0,1},{1,2},{2,3},{3,4},{4,5},{5,6},{6,7},{7,8},{8,9},{9,10},{10,1... | collective-permute-start | bytes 786440 | tf_op jit(solution)/shard_map/ppermute | solution.py:23
  441.4 8.5 %collective-permute-start.27 = (bf16[64,2048]{1,0:T(8,128)(2,1)S(1)}, bf16[64,2048]{1,0:T(8,128)(2,1)S(1)}, u32[]{:S(2)}, u32[]{:S(2)}) collective-permute-start(bf16[64,2048]{1,0:T(8,128)(2,1)S(1)} %collective-permute-done.26), channel_id=1, source_target_pairs={{0,1},{1,2},{2,3},{3,4},{4,5},{5,6},{6,7},{7,8},{8,9},{9,10},{10,1... | collective-permute-start | bytes 786440 | tf_op jit(solution)/shard_map/ppermute | solution.py:23
  449.9 8.5 %collective-permute-start.28 = (bf16[64,2048]{1,0:T(8,128)(2,1)S(1)}, bf16[64,2048]{1,0:T(8,128)(2,1)S(1)}, u32[]{:S(2)}, u32[]{:S(2)}) collective-permute-start(bf16[64,2048]{1,0:T(8,128)(2,1)S(1)} %collective-permute-done.27), channel_id=1, source_target_pairs={{0,1},{1,2},{2,3},{3,4},{4,5},{5,6},{6,7},{7,8},{8,9},{9,10},{10,1... | collective-permute-start | bytes 786440 | tf_op jit(solution)/shard_map/ppermute | solution.py:23
  458.4 8.5 %collective-permute-start.29 = (bf16[64,2048]{1,0:T(8,128)(2,1)S(1)}, bf16[64,2048]{1,0:T(8,128)(2,1)S(1)}, u32[]{:S(2)}, u32[]{:S(2)}) collective-permute-start(bf16[64,2048]{1,0:T(8,128)(2,1)S(1)} %collective-permute-done.28), channel_id=1, source_target_pairs={{0,1},{1,2},{2,3},{3,4},{4,5},{5,6},{6,7},{7,8},{8,9},{9,10},{10,1... | collective-permute-start | bytes 786440 | tf_op jit(solution)/shard_map/ppermute | solution.py:23
  467.3 5.6 %copy-start.23 = (bf16[1,512,2048]{2,1,0:T(8,128)(2,1)S(1)}, bf16[1,512,2048]{2,1,0:T(8,128)(2,1)}, u32[]{:S(2)}) copy-start(bf16[1,512,2048]{2,1,0:T(8,128)(2,1)} %param.24) | copy-start | bytes 6291460
  (9 other events, 6.3 us)
Sparse Core Ops, SparseCore 0:
  171.1 71.1 reduce-scatter.3
  265.9 72.3 reduce-scatter.5
  477.2 69.9 reduce-scatter.7
